TPU v7x, 32 devices: a whole 2x2x4 slice. The times are simulated.
32 devices in a mesh: dp: 8 (over z, x), tensor: 4 (over y, core).
Axes of the slice: x: 2, y: 2, z: 4, core: 2. Of those that a mesh axis runs over, the one named last changes fastest.
Arguments:
- tokens: bfloat16 [16384, 1024], P(('dp', 'tensor')), may hold values from -6 to 6
- condition: bfloat16 [16, 1024], P('dp'), may hold values from -6 to 6
- ada_weight: bfloat16 [1024, 6144], P(None, 'tensor'), may hold values from -0.1875 to 0.1875
- ada_bias: bfloat16 [6144], P('tensor'), may hold values from -3 to 3
- qkv_weight: bfloat16 [1024, 3, 1024], P(None, None, 'tensor'), may hold values from -0.1875 to 0.1875
- qv_bias: bfloat16 [2, 1024], P(None, 'tensor'), may hold values from -3 to 3
- proj_weight: bfloat16 [1024, 1024], P('tensor'), may hold values from -0.75 to 0.75
- proj_bias: bfloat16 [1024], replicated, may hold values from -3 to 3
- up_weight: bfloat16 [4096, 1024], P('tensor'), may hold values from -0.1875 to 0.1875
- up_bias: bfloat16 [4096], P('tensor'), may hold values from -3 to 3
- down_weight: bfloat16 [4096, 1024], P('tensor'), may hold values from -0.09375 to 0.09375
- down_bias: bfloat16 [1024], replicated, may hold values from -3 to 3
- out_grad: bfloat16 [16384, 1024], P(('dp', 'tensor')), may hold values from -6 to 6
Outputs:
- block_out: bfloat16 [16384, 1024], P(('dp', 'tensor'))
- tokens_grad: float32 [16384, 1024], P(('dp', 'tensor'))
- condition_grad: float32 [16, 1024], P('dp')
- ada_weight_grad: float32 [1024, 6144], P(None, 'tensor')
- ada_bias_grad: float32 [6144], P('tensor')
- qkv_weight_grad: float32 [1024, 3, 1024], P(None, None, 'tensor')
- qv_bias_grad: float32 [2, 1024], P(None, 'tensor')
- proj_weight_grad: float32 [1024, 1024], P('tensor')
- proj_bias_grad: float32 [1024], replicated
- up_weight_grad: float32 [4096, 1024], P('tensor')
- up_bias_grad: float32 [4096], P('tensor')
- down_weight_grad: float32 [4096, 1024], P('tensor')
- down_bias_grad: float32 [1024], replicated
All inputs are finite; a program needn't handle non-finite values.
Results may differ from a plain program's by a relative error of at most 0.023.
The roundings to bfloat16 on the way count: a program that leaves them out, or rounds other values in their place, can miss the bound.
Values may be sent and summed in bfloat16 or wider, within the bound.
No kernel may reach another device: no remote copies, remote signals or barrier semaphores. Data moves between devices by JAX's collectives and lax.ppermute only.
A program may use at most 256 MiB of HBM per device.

v0:
```python
import math
import jax
import jax.numpy as jnp
from jax import lax
from jax.sharding import PartitionSpec as P

D = 1024
HD = 64
SEQ = 1024
norm_eps = 1e-06
highest = lax.Precision.HIGHEST


def layer_norm(values):
    row_mean = jnp.mean(values, axis=-1, keepdims=True)
    centered = values - row_mean
    inv_std = lax.rsqrt(jnp.mean(centered * centered, axis=-1, keepdims=True) + norm_eps)
    return (centered * inv_std, inv_std)


def norm_back(grad_normed, normed, inv_std):
    mean_grad = jnp.mean(grad_normed, axis=-1, keepdims=True)
    mean_cross = jnp.mean(grad_normed * normed, axis=-1, keepdims=True)
    return inv_std * (grad_normed - mean_grad - normed * mean_cross)


def gelu_tanh(values):
    return jax.nn.gelu(values, approximate=True)


def attend_query(inputs):
    query_rows, kv_rows = inputs
    key_rows = kv_rows[:, 0]
    value_rows = kv_rows[:, 1]
    score_scale = 1.0 / math.sqrt(HD)
    query_count = query_rows.shape[0]
    block_rows = min(512, query_count)
    out_parts = []
    lse_parts = []
    for start_row in range(0, query_count, block_rows):
        query_blk = query_rows[start_row : start_row + block_rows]
        scores = (
            jnp.einsum("qhd,khd->hqk", query_blk, key_rows, preferred_element_type=jnp.float32)
            * score_scale
        )
        row_max = jnp.max(scores, axis=-1, keepdims=True)
        exp_scores = jnp.exp(scores - row_max)
        row_total = jnp.sum(exp_scores, axis=-1, keepdims=True)
        probs_low = (exp_scores / row_total).astype(jnp.bfloat16)
        out_parts.append(
            jnp.einsum(
                "hqk,khd->qhd", probs_low, value_rows, preferred_element_type=jnp.float32
            ).astype(jnp.bfloat16)
        )
        lse_parts.append(row_max[..., 0] + jnp.log(row_total[..., 0]))
    return (jnp.concatenate(out_parts, axis=0), jnp.concatenate(lse_parts, axis=1))


def attend_query_back(inputs):
    query_rows, kv_rows, grad_rows, lse_rows = inputs
    key_rows = kv_rows[:, 0]
    value_rows = kv_rows[:, 1]
    score_scale = 1.0 / math.sqrt(HD)
    query_count = query_rows.shape[0]
    block_rows = min(512, query_count)
    key_grad = jnp.zeros(key_rows.shape, jnp.float32)
    value_grad = jnp.zeros(value_rows.shape, jnp.float32)
    query_parts = []
    for start_row in range(0, query_count, block_rows):
        query_blk = query_rows[start_row : start_row + block_rows]
        grad_blk = grad_rows[start_row : start_row + block_rows]
        scores = (
            jnp.einsum("qhd,khd->hqk", query_blk, key_rows, preferred_element_type=jnp.float32)
            * score_scale
        )
        probs = jnp.exp(scores - lse_rows[:, start_row : start_row + block_rows, None])
        probs_low = probs.astype(jnp.bfloat16)
        value_grad = value_grad + jnp.einsum(
            "hqk,qhd->khd", probs_low, grad_blk, preferred_element_type=jnp.float32
        )
        prob_grad = jnp.einsum(
            "qhd,khd->hqk", grad_blk, value_rows, preferred_element_type=jnp.float32
        )
        row_delta = jnp.sum(probs * prob_grad, axis=-1, keepdims=True)
        score_grad = (probs * (prob_grad - row_delta)).astype(jnp.bfloat16)
        query_parts.append(
            jnp.einsum("hqk,khd->qhd", score_grad, key_rows, preferred_element_type=jnp.float32)
            * score_scale
        )
        key_grad = (
            key_grad
            + jnp.einsum("hqk,qhd->khd", score_grad, query_blk, preferred_element_type=jnp.float32)
            * score_scale
        )
    query_grad = jnp.concatenate(query_parts, axis=0)
    return (query_grad, jnp.stack([key_grad, value_grad], axis=1))


def attend_latent(packed):
    out_rows, lse_rows = attend_query((packed[:, 0], packed[:, 1:]))
    return (out_rows, lse_rows)


def attend_back(inputs):
    packed, grad_lat, lse_lat = inputs
    query_grad, kv_grad = attend_query_back((packed[:, 0], packed[:, 1:], grad_lat, lse_lat))
    return jnp.concatenate([query_grad[:, None], kv_grad], axis=1).astype(jnp.bfloat16)


def shards(
    tokens,
    condition,
    ada_weight,
    ada_bias,
    qkv_weight,
    qv_bias,
    proj_weight,
    proj_bias,
    up_weight,
    up_bias,
    down_weight,
    down_bias,
    out_grad,
):
    rows_local = tokens.shape[0]
    latents_local = condition.shape[0]
    first_row = lax.axis_index("tensor") * rows_local
    row_latent = (first_row + jnp.arange(rows_local, dtype=jnp.int32)) // SEQ
    latent_pick = (
        row_latent[:, None] == jnp.arange(latents_local, dtype=jnp.int32)[None, :]
    ).astype(jnp.float32)
    cond_wide = condition.astype(jnp.float32)
    cond_sig = jax.nn.sigmoid(cond_wide)
    silu_low = (cond_wide * cond_sig).astype(jnp.bfloat16)
    mod_cols = (
        jnp.dot(silu_low, ada_weight, preferred_element_type=jnp.float32)
        + ada_bias.astype(jnp.float32)
    ).astype(jnp.bfloat16)
    mod_all = lax.all_gather(mod_cols, "tensor", axis=1, tiled=True).astype(jnp.float32)
    mod_rows = jnp.dot(latent_pick, mod_all, precision=highest)
    shift_attn, scale_attn, gate_attn, shift_mlp, scale_mlp, gate_mlp = [
        mod_rows[:, column_set * D : (column_set + 1) * D] for column_set in range(6)
    ]
    tokens_wide = tokens.astype(jnp.float32)
    normed_attn, inv_attn = layer_norm(tokens_wide)
    attn_input = (normed_attn * (1.0 + scale_attn) + shift_attn).astype(jnp.bfloat16)
    gathered_attn = lax.all_gather(attn_input, "tensor", axis=0, tiled=True)
    head_cols = qkv_weight.shape[2]
    heads_local = head_cols // HD
    qkv_flat = qkv_weight.reshape(D, 3 * head_cols)
    qkv_shift = jnp.concatenate([qv_bias[0], jnp.zeros_like(qv_bias[0]), qv_bias[1]]).astype(
        jnp.float32
    )
    qkv_rows = (
        jnp.dot(gathered_attn, qkv_flat, preferred_element_type=jnp.float32) + qkv_shift
    ).astype(jnp.bfloat16)
    latents_group = gathered_attn.shape[0] // SEQ
    qkv_packed = qkv_rows.reshape(latents_group, SEQ, 3, heads_local, HD)
    attn_heads, attn_lse = lax.map(attend_latent, qkv_packed)
    attn_flat = attn_heads.reshape(latents_group * SEQ, head_cols)
    proj_terms = jnp.dot(attn_flat, proj_weight, preferred_element_type=jnp.float32)
    branch_attn = lax.psum_scatter(
        proj_terms.astype(jnp.bfloat16), "tensor", scatter_dimension=0, tiled=True
    ).astype(jnp.float32) + proj_bias.astype(jnp.float32)
    hidden_state = tokens_wide + gate_attn * branch_attn
    normed_mlp, inv_mlp = layer_norm(hidden_state)
    mlp_input = (normed_mlp * (1.0 + scale_mlp) + shift_mlp).astype(jnp.bfloat16)
    gathered_mlp = lax.all_gather(mlp_input, "tensor", axis=0, tiled=True)
    pre_act = jnp.einsum(
        "rd,fd->rf", gathered_mlp, up_weight, preferred_element_type=jnp.float32
    ) + up_bias.astype(jnp.float32)
    hidden_low = gelu_tanh(pre_act).astype(jnp.bfloat16)
    down_terms = jnp.dot(hidden_low, down_weight, preferred_element_type=jnp.float32)
    branch_mlp = lax.psum_scatter(
        down_terms.astype(jnp.bfloat16), "tensor", scatter_dimension=0, tiled=True
    ).astype(jnp.float32) + down_bias.astype(jnp.float32)
    block_out = (hidden_state + gate_mlp * branch_mlp).astype(jnp.bfloat16)
    grad_wide = out_grad.astype(jnp.float32)
    grad_gate_mlp = grad_wide * branch_mlp
    grad_branch_mlp = (gate_mlp * grad_wide).astype(jnp.bfloat16)
    gathered_grad = lax.all_gather(grad_branch_mlp, "tensor", axis=0, tiled=True)
    grad_hidden = jnp.einsum(
        "rd,fd->rf", gathered_grad, down_weight, preferred_element_type=jnp.float32
    )
    grad_pre = jax.vjp(gelu_tanh, pre_act)[1](grad_hidden)[0].astype(jnp.bfloat16)
    down_weight_grad = jnp.einsum(
        "rf,rd->fd", hidden_low, gathered_grad, preferred_element_type=jnp.float32
    )
    up_weight_grad = jnp.einsum(
        "rf,rd->fd", grad_pre, gathered_mlp, preferred_element_type=jnp.float32
    )
    up_bias_grad = jnp.sum(grad_pre.astype(jnp.float32), axis=0)
    input_terms = jnp.dot(grad_pre, up_weight, preferred_element_type=jnp.float32)
    grad_mlp_input = lax.psum_scatter(
        input_terms.astype(jnp.bfloat16), "tensor", scatter_dimension=0, tiled=True
    ).astype(jnp.float32)
    grad_hidden_state = grad_wide + norm_back(
        grad_mlp_input * (1.0 + scale_mlp), normed_mlp, inv_mlp
    )
    grad_branch_attn = (gate_attn * grad_hidden_state).astype(jnp.bfloat16)
    gathered_back = lax.all_gather(grad_branch_attn, "tensor", axis=0, tiled=True)
    proj_weight_grad = jnp.einsum(
        "rc,rd->cd", attn_flat, gathered_back, preferred_element_type=jnp.float32
    )
    grad_attn_flat = jnp.einsum(
        "rd,cd->rc", gathered_back, proj_weight, preferred_element_type=jnp.float32
    ).astype(jnp.bfloat16)
    grad_heads = grad_attn_flat.reshape(latents_group, SEQ, heads_local, HD)
    grad_packed = lax.map(attend_back, (qkv_packed, grad_heads, attn_lse))
    grad_qkv = grad_packed.reshape(latents_group * SEQ, 3 * head_cols)
    qkv_weight_grad = jnp.einsum(
        "rd,rc->dc", gathered_attn, grad_qkv, preferred_element_type=jnp.float32
    ).reshape(qkv_weight.shape)
    bias_sums = jnp.sum(grad_qkv.astype(jnp.float32), axis=0).reshape(3, head_cols)
    qv_bias_grad = jnp.stack([bias_sums[0], bias_sums[2]])
    attn_terms = jnp.einsum("rc,dc->rd", grad_qkv, qkv_flat, preferred_element_type=jnp.float32)
    grad_attn_input = lax.psum_scatter(
        attn_terms.astype(jnp.bfloat16), "tensor", scatter_dimension=0, tiled=True
    ).astype(jnp.float32)
    tokens_grad = grad_hidden_state + norm_back(
        grad_attn_input * (1.0 + scale_attn), normed_attn, inv_attn
    )
    grad_mod_rows = jnp.concatenate(
        [
            grad_attn_input,
            grad_attn_input * normed_attn,
            grad_hidden_state * branch_attn,
            grad_mlp_input,
            grad_mlp_input * normed_mlp,
            grad_gate_mlp,
        ],
        axis=1,
    )
    grad_mod_local = jnp.dot(latent_pick.T, grad_mod_rows, precision=highest)
    grad_mod_cols = lax.psum_scatter(
        grad_mod_local.astype(jnp.bfloat16), "tensor", scatter_dimension=1, tiled=True
    )
    ada_weight_grad = jnp.dot(silu_low.T, grad_mod_cols, preferred_element_type=jnp.float32)
    ada_bias_grad = jnp.sum(grad_mod_cols.astype(jnp.float32), axis=0)
    silu_part = jnp.dot(grad_mod_cols, ada_weight.T, preferred_element_type=jnp.float32)
    proj_bias_part = jnp.sum(grad_branch_attn.astype(jnp.float32), axis=0)
    down_bias_part = jnp.sum(grad_branch_mlp.astype(jnp.float32), axis=0)
    silu_grad, proj_bias_grad, down_bias_grad = (
        lax.psum(silu_part.astype(jnp.bfloat16), "tensor").astype(jnp.float32),
        lax.psum(proj_bias_part.astype(jnp.bfloat16), "tensor").astype(jnp.float32),
        lax.psum(down_bias_part.astype(jnp.bfloat16), "tensor").astype(jnp.float32),
    )
    condition_grad = silu_grad * (cond_sig * (1.0 + cond_wide * (1.0 - cond_sig)))
    summed = (
        lax.psum(ada_weight_grad.astype(jnp.bfloat16), "dp").astype(jnp.float32),
        lax.psum(ada_bias_grad.astype(jnp.bfloat16), "dp").astype(jnp.float32),
        lax.psum(qkv_weight_grad.astype(jnp.bfloat16), "dp").astype(jnp.float32),
        lax.psum(qv_bias_grad.astype(jnp.bfloat16), "dp").astype(jnp.float32),
        lax.psum(proj_weight_grad.astype(jnp.bfloat16), "dp").astype(jnp.float32),
        lax.psum(proj_bias_grad.astype(jnp.bfloat16), "dp").astype(jnp.float32),
        lax.psum(up_weight_grad.astype(jnp.bfloat16), "dp").astype(jnp.float32),
        lax.psum(up_bias_grad.astype(jnp.bfloat16), "dp").astype(jnp.float32),
        lax.psum(down_weight_grad.astype(jnp.bfloat16), "dp").astype(jnp.float32),
        lax.psum(down_bias_grad.astype(jnp.bfloat16), "dp").astype(jnp.float32),
    )
    return (block_out, tokens_grad, condition_grad) + tuple(summed)


def solution(mesh):
    placed = (
        P(("dp", "tensor"), None),
        P("dp", None),
        P(None, "tensor"),
        P("tensor"),
        P(None, None, "tensor"),
        P(None, "tensor"),
        P("tensor", None),
        P(),
        P("tensor", None),
        P("tensor"),
        P("tensor", None),
        P(),
        P(("dp", "tensor"), None),
    )
    return jax.shard_map(
        shards,
        mesh=mesh,
        in_specs=placed,
        out_specs=(
            P(("dp", "tensor"), None),
            P(("dp", "tensor"), None),
            P("dp", None),
            P(None, "tensor"),
            P("tensor"),
            P(None, None, "tensor"),
            P(None, "tensor"),
            P("tensor", None),
            P(),
            P("tensor", None),
            P("tensor"),
            P("tensor", None),
            P(),
        ),
        check_vma=False,
    )
```

profile of v0, /device:TPU:0, one launch (start us, length us, event | category | flops | bytes accessed | tf_op | source)
XLA Modules:
  0.0 895.3 jit_solution(1262495356426923019)
XLA Ops:
  12.4 6.3 all_gather.15
  20.6 4.5 copy-done.1
  29.8 33.0 %all-gather.5.cloned.1.call-done = bf16[2048,1024]{1,0:T(8,128)(2,1)} async-done(((bf16[512,1024]{1,0:T(8,128)(2,1)}), bf16[2048,1024]{1,0:T(8,128)(2,1)}) %all-gather.5.cloned.1.call-update) | async-done | bytes 4194320 | tf_op jit(solution)/shard_map/all_gather | solution.py:147
  62.9 7.8 add_convert_fusion
  70.7 10.1 %reshape.206 = bf16[2,1024,3,4,64]{4,3,2,1,0:T(4,128)(2,1)} reshape(bf16[2048,768]{1,0:T(8,128)(2,1)} %add_convert_fusion) | data formatting | bytes 6291456 | tf_op jit(solution)/shard_map/reshape | solution.py:158
  80.8 9.8 %copy.41 = bf16[2,1024,3,4,64]{1,4,3,2,0:T(8,128)(2,1)} copy(bf16[2,1024,3,4,64]{4,3,2,1,0:T(4,128)(2,1)} %reshape.206) | data formatting | bytes 6291456 | tf_op jit(solution)/shard_map/while | solution.py:159
  90.7 27.7 %while.22 = (s32[]{:T(128)}, bf16[2,1024,4,64]{1,3,2,0:T(8,128)(2,1)}, f32[2,4,1024]{2,1,0:T(4,128)S(1)}, bf16[2,1024,3,4,64]{1,4,3,2,0:T(8,128)(2,1)}, s32[]{:T(128)}) while((s32[]{:T(128)}, bf16[2,1024,4,64]{1,3,2,0:T(8,128)(2,1)}, f32[2,4,1024]{2,1,0:T(4,128)S(1)}, bf16[2,1024,3,4,64]{1,4,3,2,0:T(8,128)(2,1)}, s32[]{:T(128)}) %tuple.75), condition=%wide.region_7.8_spmd, body=%wide.region_2.7_spmd.sunk | while | flops 1112801280 | bytes 66224264 | solution.py:159
  126.0 44.1 %reduce-scatter.8.cloned.1.call-done = bf16[512,1024]{1,0:T(8,128)(2,1)} async-done(((bf16[2048,1024]{1,0:T(8,128)(2,1)}), bf16[512,1024]{1,0:T(8,128)(2,1)}) %reduce-scatter.8.cloned.1.call-update) | async-done | bytes 1048592 | tf_op jit(solution)/shard_map/reduce_scatter | solution.py:162
  174.1 3.7 fusion.77
  177.8 3.8 fusion.104
  181.8 30.6 %all-gather.7.cloned.1.call-done = bf16[2048,1024]{1,0:T(8,128)(2,1)} async-done(((bf16[512,1024]{1,0:T(8,128)(2,1)}), bf16[2048,1024]{1,0:T(8,128)(2,1)}) %all-gather.7.cloned.1.call-update) | async-done | bytes 4194320 | tf_op jit(solution)/shard_map/all_gather | solution.py:168
  212.4 7.1 fusion.110
  219.5 3.9 copy-done.57
  223.5 6.9 convolution_convert_fusion.5
  230.5 18.4 %all-gather.9.cloned.1.call-done = bf16[2048,1024]{1,0:T(8,128)(2,1)} async-done(((bf16[512,1024]{1,0:T(8,128)(2,1)}), bf16[2048,1024]{1,0:T(8,128)(2,1)}) %all-gather.9.cloned.1.call-update) | async-done | bytes 4194320 | tf_op jit(solution)/shard_map/all_gather | solution.py:181
  248.9 14.5 %fusion.102 = (bf16[1024]{0:T(1024)(128)(2,1)}, bf16[2048,1024]{1,0:T(8,128)(2,1)S(1)}) fusion(f32[2048,1024]{1,0:T(8,128)} %copy-done.57, f32[1024]{0:T(1024)S(1)} %convert_element_type.208, bf16[2048,1024]{1,0:T(8,128)(2,1)} %all-gather.9.cloned.1.call-done, bf16[1024,1024]{1,0:T(8,128)(2,1)} %param.27), kind=kOutput, calls=%fused_computation.184 | convolution fusion | flops 4341103616 | bytes 18880512 | tf_op jit(solution)/shard_map/rd,fd->rf/dot_general | solution.py:182
  265.4 6.0 convolution_convert_fusion.4
  272.1 24.3 %reduce-scatter.10.cloned.1.call-done = bf16[512,1024]{1,0:T(8,128)(2,1)} async-done(((bf16[2048,1024]{1,0:T(8,128)(2,1)}), bf16[512,1024]{1,0:T(8,128)(2,1)}) %reduce-scatter.10.cloned.1.call-update) | async-done | bytes 1048592 | tf_op jit(solution)/shard_map/reduce_scatter | solution.py:174
  296.4 47.6 %reduce-scatter.12.cloned.1.call-done = bf16[512,1024]{1,0:T(8,128)(2,1)} async-done(((bf16[2048,1024]{1,0:T(8,128)(2,1)}), bf16[512,1024]{1,0:T(8,128)(2,1)}) %reduce-scatter.12.cloned.1.call-update) | async-done | bytes 1048592 | tf_op jit(solution)/shard_map/reduce_scatter | solution.py:194
  344.0 5.4 fusion.83
  349.5 4.5 fusion.106
  354.1 34.6 %all-gather.11.cloned.1.call-done = bf16[2048,1024]{1,0:T(8,128)(2,1)} async-done(((bf16[512,1024]{1,0:T(8,128)(2,1)}), bf16[2048,1024]{1,0:T(8,128)(2,1)}) %all-gather.11.cloned.1.call-update) | async-done | bytes 4194320 | tf_op jit(solution)/shard_map/all_gather | solution.py:201
  388.6 4.6 convolution_convert_fusion.6
  393.2 4.4 reshape.203
  397.6 4.0 copy.45
  401.7 64.6 %while.23 = (s32[]{:T(128)}, bf16[2,1024,3,4,64]{1,4,3,2,0:T(8,128)(2,1)}, bf16[2,1024,3,4,64]{1,4,3,2,0:T(8,128)(2,1)}, f32[2,4,1024]{2,1,0:T(4,128)S(1)}, bf16...) while((s32[]{:T(128)}, bf16[2,1024,3,4,64]{1,4,3,2,0:T(8,128)(2,1)}, ...), condition=%wide.region_18.19_spmd, body=%wide.region_15.18_spmd.sunk | while | flops 2742284288 | bytes 173686992 | solution.py:209
  409.9 4.6 multiply_reduce_fusion.12
  414.4 4.6 multiply_reduce_fusion.13
  419.0 8.1 multiply_convert_fusion.8
  441.9 4.6 multiply_reduce_fusion.12
  446.5 4.6 multiply_reduce_fusion.13
  451.1 8.1 multiply_convert_fusion.8
  466.3 5.1 copy.46
  474.2 5.0 convolution_convert_fusion.3
  479.5 9.5 %convolution_convert_fusion.8 = bf16[1024,1024]{1,0:T(8,128)(2,1)} fusion(bf16[2048,1024]{1,0:T(8,128)(2,1)} %copy-done.56, bf16[2048,1024]{1,0:T(8,128)(2,1)} %all-gather.7.cloned.1.call-done), kind=kOutput, calls=%fused_computation.140 | convolution fusion | flops 4296015872 | bytes 10485760 | tf_op jit(solution)/shard_map/rf,rd->fd/dot_general | solution.py:189
  489.0 11.3 %convolution_convert_fusion.7 = bf16[1024,1024]{1,0:T(8,128)(2,1)} fusion(bf16[2048,1024]{1,0:T(8,128)(2,1)S(1)} %copy-done.53, f32[2048,1024]{1,0:T(8,128)} %copy-done.57, f32[1024]{0:T(1024)S(1)} %copy-done.47), kind=kOutput, calls=%fused_computation.139 | convolution fusion | flops 4316987392 | bytes 14684160 | tf_op jit(solution)/shard_map/rf,rd->fd/dot_general | solution.py:186
  500.3 5.1 fusion.78
  505.4 18.6 %reduce-scatter.14.cloned.1.call-done = bf16[512,1024]{1,0:T(8,128)(2,1)} async-done(((bf16[2048,1024]{1,0:T(8,128)(2,1)}), bf16[512,1024]{1,0:T(8,128)(2,1)}) %reduce-scatter.14.cloned.1.call-update) | async-done | bytes 1048592 | tf_op jit(solution)/shard_map/reduce_scatter | solution.py:217
  525.6 3.4 fusion.84
  529.1 3.5 multiply_dynamic-update-slice_fusion
  535.2 4.3 convolution_convert_fusion
  541.5 4.6 convolution_convert_fusion.9
  546.0 23.3 %reduce-scatter.16.cloned.1.call-done = bf16[1536,2]{1,0:T(8,128)(2,1)} async-done(((bf16[6144,2]{1,0:T(8,128)(2,1)}), bf16[1536,2]{1,0:T(8,128)(2,1)}) %reduce-scatter.16.cloned.1.call-update) | async-done | bytes 6160
  569.3 3.7 convolution_convert_fusion.1
  580.3 6.8 all-reduce.2
  587.2 39.6 %all-reduce = (bf16[1536]{0:T(1024)(128)(2,1)S(1)}, bf16[2,256]{1,0:T(2,128)(2,1)S(1)}, bf16[1024]{0:T(1024)(128)(2,1)S(1)}, bf16[1024]{0:T(1024)(128)(2,1)S(1)}, bf16[1024]{0:T(1024)(128)(2,1)S(1)}) all-reduce(bf16[1536]{0:T(1024)(128)(2,1)S(1)} %bitcast_reduce_fusion, ...), channel_id=1, replica_groups=mesh['dp'=8,'tensor'=4] {'dp'}, use_global_device_ids=true, to_apply=%region_26.27 | all-reduce | flops 5120 | bytes 20480 | tf_op jit(solution)/shard_map/psum | solution.py:251
  631.2 241.9 %all-reduce.5.cloned.1.call-done = (bf16[1024,1536]{1,0:T(8,128)(2,1)}, bf16[1024,3,256]{2,0,1:T(8,128)(2,1)}, bf16[256,1024]{1,0:T(8,128)(2,1)}, bf16[1024,1024]{1,0:T(8,128)(2,1)}, bf16[1024,1024]{1,0:T(8,128)(2,1)}) async-done(((bf16[1024,1536]{1,0:T(8,128)(2,1)}, bf16[1024,3,256]{2,0,1:T(8,128)(2,1)}, bf16[256,1024]{1,0:T(8,128)(2,1)}, bf16[1024,1024]{1,0:T(8,128)(2,1)}, bf16[1024,1024]{1,0:T(8,128)(2,1)}), ...) | async-done | bytes 9437200 | tf_op jit(solution)/shard_map/psum | solution.py:250
  875.2 5.6 convert_element_type.227
  (242 shorter events, 113.3 us)
Async XLA Ops:
  7.2 4.0 copy-start
  7.2 55.7 %all-gather.5.cloned.1.call-start = ((), (), s32[]{:S(2)}) async-start(), calls=%async_computation.5 | async-start | bytes 5242880 | tf_op jit(solution)/shard_map/all_gather | solution.py:147
  7.3 11.4 %copy-start.29 = (s32[512]{0:T(512)}, s32[512]{0:T(512)S(1)}, u32[]{:S(2)}) copy-start(s32[512]{0:T(512)S(1)} %add_select_fusion) | copy-start | bytes 6148
  8.9 11.7 %copy-start.33 = (f32[512]{0:T(512)}, f32[512]{0:T(512)S(1)}, u32[]{:S(2)}) copy-start(f32[512]{0:T(512)S(1)} %broadcast_multiply_fusion.5) | copy-start | bytes 6148
  10.5 10.0 %copy-start.42 = (f32[512]{0:T(512)}, f32[512]{0:T(512)S(1)}, u32[]{:S(2)}) copy-start(f32[512]{0:T(512)S(1)} %add_rsqrt_fusion.1) | copy-start | bytes 6148
  18.7 6.4 copy-start.6
  20.6 4.5 copy-start.1
  25.1 4.7 copy-start.48
  26.6 143.5 %reduce-scatter.8.cloned.1.call-start = ((), (), s32[]{:S(2)}) async-start(), calls=%async_computation.6 | async-start | bytes 5242880 | tf_op jit(solution)/shard_map/reduce_scatter | solution.py:162
  118.4 3.6 copy-start.28
  125.4 87.0 %all-gather.7.cloned.1.call-start = ((), (), s32[]{:S(2)}) async-start(), calls=%async_computation.7 | async-start | bytes 5242880 | tf_op jit(solution)/shard_map/all_gather | solution.py:168
  126.0 46.7 %copy-start.39 = (f32[1024]{0:T(1024)}, f32[1024]{0:T(1024)S(1)}, u32[]{:S(2)}) copy-start(f32[1024]{0:T(1024)S(1)} %convert_element_type.206) | copy-start | bytes 12292
  172.8 176.7 %copy-start.31 = (f32[512]{0:T(512)}, f32[512]{0:T(512)S(1)}, u32[]{:S(2)}) copy-start(f32[512]{0:T(512)S(1)} %broadcast_multiply_fusion.4) | copy-start | bytes 6148
  174.1 175.4 %copy-start.35 = (f32[512]{0:T(512)}, f32[512]{0:T(512)S(1)}, u32[]{:S(2)}) copy-start(f32[512]{0:T(512)S(1)} %add_rsqrt_fusion) | copy-start | bytes 6148
  177.7 4.0 copy-start.50
  177.8 71.1 %all-gather.9.cloned.1.call-start = ((), (), s32[]{:S(2)}) async-start(), calls=%async_computation.9 | async-start | bytes 5242880 | tf_op jit(solution)/shard_map/all_gather | solution.py:181
  181.7 114.8 %reduce-scatter.10.cloned.1.call-start = ((), (), s32[]{:S(2)}) async-start(), calls=%async_computation.8 | async-start | bytes 5242880 | tf_op jit(solution)/shard_map/reduce_scatter | solution.py:174
  181.7 67.1 %copy-start.46 = (f32[1024]{0:T(1024)}, f32[1024]{0:T(1024)S(1)}, u32[]{:S(2)}) copy-start(f32[1024]{0:T(1024)S(1)} %convert_element_type.208) | copy-start | bytes 12292
  212.4 11.1 %copy-start.54 = (bf16[1024,1024]{1,0:T(8,128)(2,1)S(1)}, bf16[1024,1024]{1,0:T(8,128)(2,1)}, u32[]{:S(2)}) copy-start(bf16[1024,1024]{1,0:T(8,128)(2,1)} %param.27) | copy-start | bytes 6291460
  219.5 3.9 copy-start.57
  230.5 113.6 %reduce-scatter.12.cloned.1.call-start = ((), (), s32[]{:S(2)}) async-start(), calls=%async_computation.10 | async-start | bytes 5242880 | tf_op jit(solution)/shard_map/reduce_scatter | solution.py:194
  248.9 16.6 %copy-start.55 = (bf16[1024,1024]{1,0:T(8,128)(2,1)S(1)}, bf16[1024,1024]{1,0:T(8,128)(2,1)}, u32[]{:S(2)}) copy-start(bf16[1024,1024]{1,0:T(8,128)(2,1)} %param.25) | copy-start | bytes 6291460
  271.5 117.2 %all-gather.11.cloned.1.call-start = ((), (), s32[]{:S(2)}) async-start(), calls=%async_computation.11 | async-start | bytes 5242880 | tf_op jit(solution)/shard_map/all_gather | solution.py:201
  272.1 77.3 %copy-start.37 = (f32[1024]{0:T(1024)}, f32[1024]{0:T(1024)S(1)}, u32[]{:S(2)}) copy-start(f32[1024]{0:T(1024)S(1)} %convert_element_type.212) | copy-start | bytes 12292
  344.0 5.5 copy-start.3
  344.0 5.5 copy-start.8
  344.0 5.5 copy-start.13
  354.0 169.9 %reduce-scatter.14.cloned.1.call-start = ((), (), s32[]{:S(2)}) async-start(), calls=%async_computation.12 | async-start | bytes 5242880 | tf_op jit(solution)/shard_map/reduce_scatter | solution.py:217
  479.2 9.8 %copy-start.47 = (f32[1024]{0:T(1024)S(1)}, f32[1024]{0:T(1024)}, u32[]{:S(2)}) copy-start(f32[1024]{0:T(1024)} %copy-done.46) | copy-start | bytes 12292
  479.2 90.1 %reduce-scatter.16.cloned.1.call-start = ((), (), s32[]{:S(2)}) async-start(), calls=%async_computation.13 | async-start | bytes 1966080
  479.5 9.5 %copy-start.53 = (bf16[2048,1024]{1,0:T(8,128)(2,1)S(1)}, bf16[2048,1024]{1,0:T(8,128)(2,1)}, u32[]{:S(2)}) copy-start(bf16[2048,1024]{1,0:T(8,128)(2,1)} %all-gather.9.cloned.1.call-done) | copy-start | bytes 12582916
  489.0 11.3 %copy-start.21 = (bf16[96,8,2,1024]{3,1,2,0:T(8,128)(2,1)S(1)}, bf16[96,8,2,1024]{3,1,2,0:T(8,128)(2,1)}, u32[]{:S(2)}) copy-start(bf16[96,8,2,1024]{3,1,2,0:T(8,128)(2,1)} %copy-done.20) | copy-start | bytes 9437188
  489.0 11.3 %copy-start.52 = (bf16[2048,1024]{1,0:T(8,128)(2,1)S(1)}, bf16[2048,1024]{1,0:T(8,128)(2,1)}, u32[]{:S(2)}) copy-start(bf16[2048,1024]{1,0:T(8,128)(2,1)} %all-gather.5.cloned.1.call-done) | copy-start | bytes 12582916
  500.3 25.3 %copy-start.34 = (f32[512]{0:T(512)S(1)}, f32[512]{0:T(512)}, u32[]{:S(2)}) copy-start(f32[512]{0:T(512)} %copy-done.33) | copy-start | bytes 6148
  500.3 25.3 %copy-start.43 = (f32[512]{0:T(512)S(1)}, f32[512]{0:T(512)}, u32[]{:S(2)}) copy-start(f32[512]{0:T(512)} %copy-done.42) | copy-start | bytes 6148
  505.4 23.6 %copy-start.40 = (f32[1024]{0:T(1024)S(1)}, f32[1024]{0:T(1024)}, u32[]{:S(2)}) copy-start(f32[1024]{0:T(1024)} %copy-done.39) | copy-start | bytes 12292
  523.9 5.1 copy-start.7
  523.9 5.1 copy-start.12
  523.9 5.1 copy-start.15
  523.9 5.1 copy-start.17
  529.1 3.8 copy-start.32
  529.1 3.8 copy-start.36
  541.1 28.2 %copy-start.41 = (bf16[2,1024]{1,0:T(2,128)(2,1)S(1)}, bf16[2,1024]{1,0:T(2,128)(2,1)}, u32[]{:S(2)}) copy-start(bf16[2,1024]{1,0:T(2,128)(2,1)} %param.18) | copy-start | bytes 12292
  541.1 331.9 %all-reduce.5.cloned.1.call-start = ((), (), s32[]{:S(2)}) async-start(), calls=%async_computation.14 | async-start | bytes 18874368 | tf_op jit(solution)/shard_map/psum | solution.py:250
  573.0 6.4 copy-start.19
  573.0 7.3 copy-start.44
  573.0 7.2 copy-start.45
  875.2 5.6 copy-start.25
  (25 other events, 44.4 us)
Sparse Core Ops, SparseCore 0:
  26.7 36.1 all-gather.4
  125.5 44.5 reduce-scatter.7
  177.9 34.4 all-gather.6
  214.4 34.4 all-gather.8
  251.8 44.5 reduce-scatter.9
  299.4 44.5 reduce-scatter.11
  354.1 34.4 all-gather.10
  479.3 44.5 reduce-scatter.13
  541.2 28.0 reduce-scatter.15
  574.5 298.5 all-reduce.4
where the time goes:
time: 900 us; the launch traced here: 895 us
  waiting for transfers between devices  516 us (57%)
  matrix products  152 us (17%)
  other arithmetic  82.5 us (9%)
  local copies, waits for them, and re-layouts  73.8 us (8%)
  blocking collectives  52.7 us (6%)
  between operations  15 us (2%)
    psum x1, waiting for transfers between devices, shards(): lax.psum(ada_weight_grad.astype(jnp.bfloat16), 'dp').astype(jnp.float32)  242 us
    reduce_scatter x1, waiting for transfers between devices, shards(): lax.psum_scatter(input_terms.astype(jnp.bfloat16), 'tensor', scatter_dime...  47.6 us
    reduce_scatter x1, waiting for transfers between devices, shards(): lax.psum_scatter(proj_terms.astype(jnp.bfloat16), 'tensor', scatter_dimen...  44.1 us
    psum x1, blocking collectives, shards(): lax.psum(ada_bias_grad.astype(jnp.bfloat16), 'dp').astype(jnp.float32)  39.6 us
    all_gather x1, waiting for transfers between devices, shards(): lax.all_gather(grad_branch_attn, 'tensor', axis=0, tiled=True)  34.6 us
    all_gather x1, waiting for transfers between devices, shards(): gathered_attn = lax.all_gather(attn_input, 'tensor', axis=0, tiled=True)  33 us
    all_gather x1, waiting for transfers between devices, shards(): gathered_mlp = lax.all_gather(mlp_input, 'tensor', axis=0, tiled=True)  30.6 us
    reduce_scatter x1, waiting for transfers between devices, shards(): lax.psum_scatter(down_terms.astype(jnp.bfloat16), 'tensor', scatter_dimen...  24.3 us
  transfers between devices with their start and end apart: 10, of which 10 were waited for; matrix products, arithmetic and copies ran while one was open for 9% of the time, Pallas kernels for 0%

commit v1 on v0

--- a/solution.py
+++ b/solution.py
@@ -246,8 +246,13 @@
         lax.psum(down_bias_part.astype(jnp.bfloat16), "tensor").astype(jnp.float32),
     )
     condition_grad = silu_grad * (cond_sig * (1.0 + cond_wide * (1.0 - cond_sig)))
+
+    def frame_number(local_x, mesh_name):
+        inter = jnp.sum(lax.all_gather(local_x, mesh_name), 0)
+        return inter
+
     summed = (
-        lax.psum(ada_weight_grad.astype(jnp.bfloat16), "dp").astype(jnp.float32),
+        frame_number(ada_weight_grad.astype(jnp.bfloat16), "dp").astype(jnp.float32),
         lax.psum(ada_bias_grad.astype(jnp.bfloat16), "dp").astype(jnp.float32),
         lax.psum(qkv_weight_grad.astype(jnp.bfloat16), "dp").astype(jnp.float32),
         lax.psum(qv_bias_grad.astype(jnp.bfloat16), "dp").astype(jnp.float32),

time: 900 us -> 1300 us (1.44)
  waiting for transfers between devices: 516 us -> 884 us
  blocking collectives: 52.7 us -> 72.1 us
  other arithmetic: 82.5 us -> 98.7 us
    all_gather x0 -> x1, waiting for transfers between devices: none -> 401 us  [frame_number(): inter = jnp.sum(lax.all_gather(local_x, mesh_name), 0)]
    psum x1, waiting for transfers between devices: 242 us -> 208 us  [shards(): lax.psum(qkv_weight_grad.astype(jnp.bfloat16), 'dp').astype(jnp.float32)]
    psum x1, blocking collectives: 39.6 us -> 58.4 us  [shards(): lax.psum(ada_bias_grad.astype(jnp.bfloat16), 'dp').astype(jnp.float32)]
    reduce_sum x0 -> x1, other arithmetic: none -> 15.5 us  [frame_number(): inter = jnp.sum(lax.all_gather(local_x, mesh_name), 0)]
  transfers between devices with their start and end apart: 10 -> 11, of which waited for: 10 -> 11; matrix products, arithmetic and copies ran while one was open for 9% -> 7% of each run, Pallas kernels for 0% -> 0%
where the time goes in v1:
time: 1300 us
  waiting for transfers between devices  884 us (68%)
  matrix products  152 us (12%)
  other arithmetic  98.7 us (8%)
  blocking collectives  72.1 us (6%)
  local copies, waits for them, and re-layouts  70.8 us (5%)
  between operations  14.7 us (1%)
    all_gather x1, waiting for transfers between devices, frame_number(): inter = jnp.sum(lax.all_gather(local_x, mesh_name), 0)  401 us
    psum x1, waiting for transfers between devices, shards(): lax.psum(qkv_weight_grad.astype(jnp.bfloat16), 'dp').astype(jnp.float32)  208 us
    psum x1, blocking collectives, shards(): lax.psum(ada_bias_grad.astype(jnp.bfloat16), 'dp').astype(jnp.float32)  58.4 us
    reduce_scatter x1, waiting for transfers between devices, shards(): lax.psum_scatter(input_terms.astype(jnp.bfloat16), 'tensor', scatter_dime...  47.6 us
    reduce_scatter x1, waiting for transfers between devices, shards(): lax.psum_scatter(proj_terms.astype(jnp.bfloat16), 'tensor', scatter_dimen...  44.1 us
    all_gather x1, waiting for transfers between devices, shards(): lax.all_gather(grad_branch_attn, 'tensor', axis=0, tiled=True)  34.6 us
    all_gather x1, waiting for transfers between devices, shards(): gathered_attn = lax.all_gather(attn_input, 'tensor', axis=0, tiled=True)  33 us
    all_gather x1, waiting for transfers between devices, shards(): gathered_mlp = lax.all_gather(mlp_input, 'tensor', axis=0, tiled=True)  30.6 us
  transfers between devices with their start and end apart: 11, of which 11 were waited for; matrix products, arithmetic and copies ran while one was open for 7% of the time, Pallas kernels for 0%

profile of v1, /device:TPU:0, one launch (start us, length us, event | category | flops | bytes accessed | tf_op | source)
XLA Modules:
  0.0 1295.1 jit_solution(1730815581424835026)
XLA Ops:
  12.4 6.3 all_gather.21
  20.6 4.5 copy-done.1
  29.8 33.0 %all-gather.7.cloned.1.call-done = bf16[2048,1024]{1,0:T(8,128)(2,1)} async-done(((bf16[512,1024]{1,0:T(8,128)(2,1)}), bf16[2048,1024]{1,0:T(8,128)(2,1)}) %all-gather.7.cloned.1.call-update) | async-done | bytes 4194320 | tf_op jit(solution)/shard_map/all_gather | solution.py:147
  62.9 7.8 add_convert_fusion
  70.7 10.1 reshape.207
  80.8 9.8 copy.41
  90.7 27.7 %while.22 = (s32[]{:T(128)}, bf16[2,1024,4,64]{1,3,2,0:T(8,128)(2,1)}, f32[2,4,1024]{2,1,0:T(4,128)S(1)}, bf16[2,1024,3,4,64]{1,4,3,2,0:T(8,128)(2,1)}, s32[]{:T(128)}) while((s32[]{:T(128)}, bf16[2,1024,4,64]{1,3,2,0:T(8,128)(2,1)}, f32[2,4,1024]{2,1,0:T(4,128)S(1)}, bf16[2,1024,3,4,64]{1,4,3,2,0:T(8,128)(2,1)}, s32[]{:T(128)}) %tuple.75), condition=%wide.region_7.8_spmd, body=%wide.region_2.7_spmd.sunk | while | flops 1112801280 | bytes 66224264 | solution.py:159
  126.0 44.1 %reduce-scatter.8.cloned.1.call-done = bf16[512,1024]{1,0:T(8,128)(2,1)} async-done(((bf16[2048,1024]{1,0:T(8,128)(2,1)}), bf16[512,1024]{1,0:T(8,128)(2,1)}) %reduce-scatter.8.cloned.1.call-update) | async-done | bytes 1048592 | tf_op jit(solution)/shard_map/reduce_scatter | solution.py:162
  174.1 3.7 fusion.77
  177.8 3.8 fusion.104
  181.8 30.6 %all-gather.9.cloned.1.call-done = bf16[2048,1024]{1,0:T(8,128)(2,1)} async-done(((bf16[512,1024]{1,0:T(8,128)(2,1)}), bf16[2048,1024]{1,0:T(8,128)(2,1)}) %all-gather.9.cloned.1.call-update) | async-done | bytes 4194320 | tf_op jit(solution)/shard_map/all_gather | solution.py:168
  212.4 7.1 fusion.110
  219.5 3.9 copy-done.56
  223.5 6.9 convolution_convert_fusion.5
  230.5 18.4 %all-gather.11.cloned.1.call-done = bf16[2048,1024]{1,0:T(8,128)(2,1)} async-done(((bf16[512,1024]{1,0:T(8,128)(2,1)}), bf16[2048,1024]{1,0:T(8,128)(2,1)}) %all-gather.11.cloned.1.call-update) | async-done | bytes 4194320 | tf_op jit(solution)/shard_map/all_gather | solution.py:181
  248.9 14.5 %fusion.102 = (bf16[1024]{0:T(1024)(128)(2,1)}, bf16[2048,1024]{1,0:T(8,128)(2,1)S(1)}) fusion(f32[2048,1024]{1,0:T(8,128)} %copy-done.56, f32[1024]{0:T(1024)S(1)} %convert_element_type.210, bf16[2048,1024]{1,0:T(8,128)(2,1)} %all-gather.11.cloned.1.call-done, bf16[1024,1024]{1,0:T(8,128)(2,1)} %param.27), kind=kOutput, calls=%fused_computation.184 | convolution fusion | flops 4341103616 | bytes 18880512 | tf_op jit(solution)/shard_map/rd,fd->rf/dot_general | solution.py:182
  265.4 6.0 convolution_convert_fusion.4
  272.1 24.3 %reduce-scatter.10.cloned.1.call-done = bf16[512,1024]{1,0:T(8,128)(2,1)} async-done(((bf16[2048,1024]{1,0:T(8,128)(2,1)}), bf16[512,1024]{1,0:T(8,128)(2,1)}) %reduce-scatter.10.cloned.1.call-update) | async-done | bytes 1048592 | tf_op jit(solution)/shard_map/reduce_scatter | solution.py:174
  296.4 47.6 %reduce-scatter.12.cloned.1.call-done = bf16[512,1024]{1,0:T(8,128)(2,1)} async-done(((bf16[2048,1024]{1,0:T(8,128)(2,1)}), bf16[512,1024]{1,0:T(8,128)(2,1)}) %reduce-scatter.12.cloned.1.call-update) | async-done | bytes 1048592 | tf_op jit(solution)/shard_map/reduce_scatter | solution.py:194
  344.0 5.4 fusion.83
  349.5 4.5 fusion.106
  354.0 34.6 %all-gather.13.cloned.1.call-done = bf16[2048,1024]{1,0:T(8,128)(2,1)} async-done(((bf16[512,1024]{1,0:T(8,128)(2,1)}), bf16[2048,1024]{1,0:T(8,128)(2,1)}) %all-gather.13.cloned.1.call-update) | async-done | bytes 4194320 | tf_op jit(solution)/shard_map/all_gather | solution.py:201
  388.6 4.6 convolution_convert_fusion.6
  393.2 4.4 reshape.204
  397.6 4.0 copy.45
  401.6 64.6 %while.23 = (s32[]{:T(128)}, bf16[2,1024,3,4,64]{1,4,3,2,0:T(8,128)(2,1)}, bf16[2,1024,3,4,64]{1,4,3,2,0:T(8,128)(2,1)}, f32[2,4,1024]{2,1,0:T(4,128)S(1)}, bf16...) while((s32[]{:T(128)}, bf16[2,1024,3,4,64]{1,4,3,2,0:T(8,128)(2,1)}, ...), condition=%wide.region_18.19_spmd, body=%wide.region_15.18_spmd.sunk | while | flops 2742284288 | bytes 173686992 | solution.py:209
  409.8 4.5 multiply_reduce_fusion.12
  414.4 4.6 multiply_reduce_fusion.13
  419.0 8.1 multiply_convert_fusion.8
  441.9 4.5 multiply_reduce_fusion.12
  446.4 4.6 multiply_reduce_fusion.13
  451.0 8.1 multiply_convert_fusion.8
  466.2 5.1 copy.46
  474.1 5.0 convolution_convert_fusion.3
  479.4 9.6 convolution_convert_fusion.8
  489.0 11.3 convolution_convert_fusion.7
  500.3 5.0 fusion.78
  505.3 18.5 %reduce-scatter.14.cloned.1.call-done = bf16[512,1024]{1,0:T(8,128)(2,1)} async-done(((bf16[2048,1024]{1,0:T(8,128)(2,1)}), bf16[512,1024]{1,0:T(8,128)(2,1)}) %reduce-scatter.14.cloned.1.call-update) | async-done | bytes 1048592 | tf_op jit(solution)/shard_map/reduce_scatter | solution.py:217
  535.1 4.3 convolution_convert_fusion
  541.1 4.6 convolution_convert_fusion.9
  546.0 23.2 %reduce-scatter.16.cloned.1.call-done = bf16[1536,2]{1,0:T(8,128)(2,1)} async-done(((bf16[6144,2]{1,0:T(8,128)(2,1)}), bf16[1536,2]{1,0:T(8,128)(2,1)}) %reduce-scatter.16.cloned.1.call-update) | async-done | bytes 6160
  569.2 3.7 convolution_convert_fusion.1
  576.1 208.4 %all-reduce.5.cloned.1.call-done = (bf16[1024,3,256]{2,0,1:T(8,128)(2,1)}, bf16[256,1024]{1,0:T(8,128)(2,1)}, bf16[1024,1024]{1,0:T(8,128)(2,1)}, bf16[1024,1024]{1,0:T(8,128)(2,1)}) async-done(((bf16[1024,3,256]{2,0,1:T(8,128)(2,1)}, bf16[256,1024]{1,0:T(8,128)(2,1)}, bf16[1024,1024]{1,0:T(8,128)(2,1)}, bf16[1024,1024]{1,0:T(8,128)(2,1)}), (bf16[1024,3,256]{2,0,1:T(8,128)(2,1)}, ...) | async-done | bytes 6291472 | tf_op jit(solution)/shard_map/psum | solution.py:257
  796.0 7.3 all-reduce.2
  803.5 58.4 %all-reduce = (bf16[1536]{0:T(1024)(128)(2,1)S(1)}, bf16[2,256]{1,0:T(2,128)(2,1)S(1)}, bf16[1024]{0:T(1024)(128)(2,1)S(1)}, bf16[1024]{0:T(1024)(128)(2,1)S(1)}, bf16[1024]{0:T(1024)(128)(2,1)S(1)}) all-reduce(bf16[1536]{0:T(1024)(128)(2,1)S(1)} %bitcast_reduce_fusion, ...), channel_id=1, replica_groups=mesh['dp'=8,'tensor'=4] {'dp'}, use_global_device_ids=true, to_apply=%region_26.27 | all-reduce | flops 5120 | bytes 20480 | tf_op jit(solution)/shard_map/psum | solution.py:256
  866.2 401.0 %all-gather.15.cloned.1.call-done = bf16[8192,1536]{1,0:T(8,128)(2,1)} async-done(((bf16[1024,1536]{1,0:T(8,128)(2,1)}), bf16[8192,1536]{1,0:T(8,128)(2,1)}) %all-gather.15.cloned.1.call-update) | async-done | bytes 25165840 | tf_op jit(solution)/shard_map/all_gather | solution.py:251
  1267.3 15.5 %reduce_sum.185 = bf16[1024,1536]{1,0:T(8,128)(2,1)} reduce(bf16[8,1024,1536]{2,1,0:T(8,128)(2,1)} %bitcast.217, bf16[]{:T(256)} %constant.87.clone.1), dimensions={0}, to_apply=%region_24.25 | reduce | flops 11010048 | bytes 28311554 | tf_op jit(solution)/shard_map/reduce_sum | solution.py:251
  1282.8 5.5 convert_element_type.229
  (244 shorter events, 118.2 us)
Async XLA Ops:
  7.2 4.0 copy-start
  7.2 55.7 %all-gather.7.cloned.1.call-start = ((), (), s32[]{:S(2)}) async-start(), calls=%async_computation.5 | async-start | bytes 5242880 | tf_op jit(solution)/shard_map/all_gather | solution.py:147
  7.3 11.4 copy-start.28
  8.9 11.7 copy-start.32
  10.5 10.0 copy-start.41
  18.7 6.4 copy-start.6
  20.6 4.5 copy-start.1
  25.1 4.7 copy-start.47
  26.6 143.5 %reduce-scatter.8.cloned.1.call-start = ((), (), s32[]{:S(2)}) async-start(), calls=%async_computation.6 | async-start | bytes 5242880 | tf_op jit(solution)/shard_map/reduce_scatter | solution.py:162
  118.4 3.7 copy-start.27
  125.4 87.0 %all-gather.9.cloned.1.call-start = ((), (), s32[]{:S(2)}) async-start(), calls=%async_computation.7 | async-start | bytes 5242880 | tf_op jit(solution)/shard_map/all_gather | solution.py:168
  126.0 46.7 %copy-start.38 = (f32[1024]{0:T(1024)}, f32[1024]{0:T(1024)S(1)}, u32[]{:S(2)}) copy-start(f32[1024]{0:T(1024)S(1)} %convert_element_type.208) | copy-start | bytes 12292
  172.8 176.6 %copy-start.30 = (f32[512]{0:T(512)}, f32[512]{0:T(512)S(1)}, u32[]{:S(2)}) copy-start(f32[512]{0:T(512)S(1)} %broadcast_multiply_fusion.4) | copy-start | bytes 6148
  174.1 175.3 %copy-start.34 = (f32[512]{0:T(512)}, f32[512]{0:T(512)S(1)}, u32[]{:S(2)}) copy-start(f32[512]{0:T(512)S(1)} %add_rsqrt_fusion) | copy-start | bytes 6148
  177.7 4.0 copy-start.49
  177.8 71.1 %all-gather.11.cloned.1.call-start = ((), (), s32[]{:S(2)}) async-start(), calls=%async_computation.9 | async-start | bytes 5242880 | tf_op jit(solution)/shard_map/all_gather | solution.py:181
  181.7 114.7 %reduce-scatter.10.cloned.1.call-start = ((), (), s32[]{:S(2)}) async-start(), calls=%async_computation.8 | async-start | bytes 5242880 | tf_op jit(solution)/shard_map/reduce_scatter | solution.py:174
  181.8 67.1 %copy-start.45 = (f32[1024]{0:T(1024)}, f32[1024]{0:T(1024)S(1)}, u32[]{:S(2)}) copy-start(f32[1024]{0:T(1024)S(1)} %convert_element_type.210) | copy-start | bytes 12292
  212.4 11.1 copy-start.53
  219.5 3.9 copy-start.56
  230.5 113.5 %reduce-scatter.12.cloned.1.call-start = ((), (), s32[]{:S(2)}) async-start(), calls=%async_computation.10 | async-start | bytes 5242880 | tf_op jit(solution)/shard_map/reduce_scatter | solution.py:194
  248.9 16.6 %copy-start.54 = (bf16[1024,1024]{1,0:T(8,128)(2,1)S(1)}, bf16[1024,1024]{1,0:T(8,128)(2,1)}, u32[]{:S(2)}) copy-start(bf16[1024,1024]{1,0:T(8,128)(2,1)} %param.25) | copy-start | bytes 6291460
  271.4 117.2 %all-gather.13.cloned.1.call-start = ((), (), s32[]{:S(2)}) async-start(), calls=%async_computation.11 | async-start | bytes 5242880 | tf_op jit(solution)/shard_map/all_gather | solution.py:201
  272.1 77.3 %copy-start.36 = (f32[1024]{0:T(1024)}, f32[1024]{0:T(1024)S(1)}, u32[]{:S(2)}) copy-start(f32[1024]{0:T(1024)S(1)} %convert_element_type.214) | copy-start | bytes 12292
  344.0 5.5 copy-start.3
  344.0 5.5 copy-start.8
  344.0 5.5 copy-start.13
  354.0 169.9 %reduce-scatter.14.cloned.1.call-start = ((), (), s32[]{:S(2)}) async-start(), calls=%async_computation.12 | async-start | bytes 5242880 | tf_op jit(solution)/shard_map/reduce_scatter | solution.py:217
  479.1 9.9 copy-start.46
  479.2 90.1 %reduce-scatter.16.cloned.1.call-start = ((), (), s32[]{:S(2)}) async-start(), calls=%async_computation.14 | async-start | bytes 1966080
  479.4 9.6 copy-start.52
  489.0 11.3 copy-start.21
  489.0 11.3 copy-start.51
  500.3 25.2 %copy-start.33 = (f32[512]{0:T(512)S(1)}, f32[512]{0:T(512)}, u32[]{:S(2)}) copy-start(f32[512]{0:T(512)} %copy-done.32) | copy-start | bytes 6148
  500.3 25.2 %copy-start.42 = (f32[512]{0:T(512)S(1)}, f32[512]{0:T(512)}, u32[]{:S(2)}) copy-start(f32[512]{0:T(512)} %copy-done.41) | copy-start | bytes 6148
  505.3 23.6 %copy-start.39 = (f32[1024]{0:T(1024)S(1)}, f32[1024]{0:T(1024)}, u32[]{:S(2)}) copy-start(f32[1024]{0:T(1024)} %copy-done.38) | copy-start | bytes 12292
  523.9 5.1 copy-start.7
  523.9 5.1 copy-start.12
  523.9 5.1 copy-start.15
  523.9 5.1 copy-start.17
  529.0 3.6 copy-start.9
  529.0 3.8 copy-start.31
  529.0 3.8 copy-start.35
  541.1 243.4 %all-reduce.5.cloned.1.call-start = ((), (), s32[]{:S(2)}) async-start(), calls=%async_computation.15 | async-start | bytes 12582912 | tf_op jit(solution)/shard_map/psum | solution.py:257
  545.7 23.5 %copy-start.40 = (bf16[2,1024]{1,0:T(2,128)(2,1)S(1)}, bf16[2,1024]{1,0:T(2,128)(2,1)}, u32[]{:S(2)}) copy-start(bf16[2,1024]{1,0:T(2,128)(2,1)} %param.18) | copy-start | bytes 12292
  545.7 721.6 %all-gather.15.cloned.1.call-start = ((), (), s32[]{:S(2)}) async-start(), calls=%async_computation.13 | async-start | bytes 28311552 | tf_op jit(solution)/shard_map/all_gather | solution.py:251
  784.5 5.6 copy-start.23
  792.6 3.4 copy-start.44
  (25 other events, 43.8 us)
Sparse Core Ops, SparseCore 0:
  26.7 36.1 all-gather.6
  125.5 44.5 reduce-scatter.7
  177.9 34.4 all-gather.8
  214.4 34.4 all-gather.10
  251.8 44.5 reduce-scatter.9
  299.4 44.5 reduce-scatter.11
  354.1 34.4 all-gather.12
  479.3 44.5 reduce-scatter.13
  541.2 27.9 reduce-scatter.15
  574.1 210.3 all-reduce.4
  786.6 480.6 all-gather.14
